TPU v7x, 512 devices: a whole 4x8x8 slice. The times are simulated.
512 devices in a mesh: box: 128 (over z, y, core), col: 4 (over x).
Axes of the slice: x: 4, y: 8, z: 8, core: 2. Of those that a mesh axis runs over, the one named last changes fastest.
Arguments:
- basis: float32 [4, 2, 64, 65536], P(None, None, 'col', 'box'), may hold values from -1000 to 1000
- offsets: float32 [3, 65536], P(None, 'box'), may hold values from -0.5 to 0.5
- weights: float32 [65536], P('box'), may hold values from 0.03 to 0.3
- interp: float32 [512, 32, 128], P('box'), may hold values from 0 to 1
- skeleton: int32 [512, 32], P('box'), may hold values from 0 to 127, as said below
- near_boxes: int32 [512, 27], P('box'), may hold values from 0 to 511, as said below
- near_count: int32 [512], P('box'), may hold values from 3 to 27, as said below
Outputs:
- new_block: float32 [2, 64, 65536], P(None, 'col', 'box')
- coupling: float32 [4, 64, 64], replicated
- factor: float32 [64, 64], replicated
Inputs may be any that keep to these rules, and one draw needn't show every extreme that they name: `skeleton`: each row holds 32 different points of the box. `near_boxes`: entry 0 of box b's row is b itself, entry 1 is b + 4 and entry 2 is b - 4, both clipped to the boxes; every entry lies within 4 boxes of b. Box b's near field is the first near_count[b] entries of its row of near_boxes.
All inputs are finite; a program needn't handle non-finite values.
Results may differ from a plain program's by a relative error of at most 0.0003.
Values sent between devices are 32-bit elements; how exact they have to be, the bound alone decides.
No kernel may reach another device: no remote copies, remote signals or barrier semaphores. Data moves between devices by JAX's collectives and lax.ppermute only.
A program may use at most 64 MiB of HBM per device.

v0:
```python
import math
import jax
import jax.numpy as jnp
from jax import lax
from jax.sharding import PartitionSpec as P

BOX_DEV = 4
WAVENUMBER = 6.0
SMOOTHING = 0.1
SHIFT_SCALE = 0.02
EPSILON = 1e-06
HIGHEST = lax.Precision.HIGHEST
SOURCE_BLOCK = 2048


def extended_2(cells, sides, width):
    for axis, dim in sides:
        count = lax.axis_size(axis)
        ends = count - 1
        head = lax.slice_in_dim(cells, 0, width, axis=dim)
        tail = lax.slice_in_dim(cells, cells.shape[dim] - width, cells.shape[dim], axis=dim)
        cells = jnp.concatenate(
            [
                lax.ppermute(tail, axis, [(i, (i + 1) % count) for i in range(ends)]),
                cells,
                lax.ppermute(head, axis, [((i + 1) % count, i) for i in range(ends)]),
            ],
            axis=dim,
        )
    return cells


def box_centers(box_index):
    along_band = (box_index // BOX_DEV).astype(jnp.float32)
    across = (box_index % BOX_DEV).astype(jnp.float32)
    return jnp.stack([along_band, across, jnp.zeros_like(along_band)])


def helmholtz_pair(targets, sources):
    spread = SMOOTHING * SMOOTHING
    for axis_index in range(3):
        spread = (
            spread + (targets[axis_index][..., :, None] - sources[axis_index][..., None, :]) ** 2
        )
    distance = jnp.sqrt(spread)
    factor = 1.0 / (4.0 * math.pi * distance)
    return (jnp.cos(WAVENUMBER * distance) * factor, jnp.sin(WAVENUMBER * distance) * factor)


def far_block(skel_count, target_pos, target_weight, running, shard_piece, first_row):
    value_rows = shard_piece.shape[0] - 3
    source_count = shard_piece.shape[1]
    source_boxes = source_count // skel_count
    target_count = target_pos.shape[1]
    box_weight = lax.dynamic_slice_in_dim(target_weight, first_row // skel_count, source_boxes, 1)
    kernel_re, kernel_im = helmholtz_pair(target_pos, shard_piece[value_rows:])
    kernel_re = (
        kernel_re.reshape(target_count, source_boxes, skel_count) * box_weight[:, :, None]
    ).reshape(target_count, source_count)
    kernel_im = (
        kernel_im.reshape(target_count, source_boxes, skel_count) * box_weight[:, :, None]
    ).reshape(target_count, source_count)
    stacked = jnp.stack([kernel_re, kernel_im])
    charge_rows = shard_piece[:value_rows].reshape(2, value_rows // 2, source_count)
    product = jnp.einsum("gts,pcs->gpct", stacked, charge_rows, precision=HIGHEST)
    return running + jnp.stack([product[0, 0] - product[1, 1], product[1, 0] + product[0, 1]])


def far_fold(skel_count, target_pos, target_weight, running, shard_piece):
    source_count = shard_piece.shape[1]

    def one_block(block_index, carry):
        offset = block_index * SOURCE_BLOCK
        block_piece = lax.dynamic_slice_in_dim(shard_piece, offset, SOURCE_BLOCK, 1)
        return far_block(skel_count, target_pos, target_weight, carry, block_piece, offset)

    return lax.fori_loop(0, source_count // SOURCE_BLOCK, one_block, running)


def shards(basis, offsets, weights, interp, skeleton, near_boxes, near_count):
    box_count = near_count.shape[0]
    points = interp.shape[2]
    skel_count = interp.shape[1]
    slot_count = near_boxes.shape[1]
    prior_blocks = basis.shape[0]
    columns = basis.shape[2]
    total_boxes = box_count * lax.axis_size("box")
    first_box = lax.axis_index("box") * box_count
    own_boxes = first_box + jnp.arange(box_count, dtype=jnp.int32)
    positions = offsets.reshape(3, box_count, points) + box_centers(own_boxes)[:, :, None]
    current = basis[prior_blocks - 1]
    sources = (current * weights).reshape(2, columns, box_count, points)
    payload = jnp.concatenate([sources.reshape(2 * columns, box_count, points), positions], axis=0)
    extended = extended_2(payload, (("box", 1),), box_count)

    def near_slot(slot_index, running):
        listed = lax.dynamic_index_in_dim(near_boxes, slot_index, 1, keepdims=False)
        live_slot = (slot_index < near_count).astype(jnp.float32)
        picked = jnp.take(extended, listed - first_box + box_count, axis=1)
        source_pos = picked[2 * columns :]
        source_val = (picked[: 2 * columns] * live_slot[None, :, None]).reshape(
            2, columns, box_count, points
        )
        kernel_re, kernel_im = helmholtz_pair(positions, source_pos)
        stacked = jnp.stack([kernel_re, kernel_im])
        product = jnp.einsum("gbtq,pcbq->gpcbt", stacked, source_val, precision=HIGHEST)
        return running + jnp.stack([product[0, 0] - product[1, 1], product[1, 0] + product[0, 1]])

    near_init = jnp.zeros((2, columns, box_count, points), jnp.float32)
    near_field = lax.fori_loop(0, slot_count, near_slot, near_init)
    charges = jnp.einsum("bkq,pcbq->pcbk", interp, sources, precision=HIGHEST).reshape(
        2, columns, box_count * skel_count
    )
    skel_pos = jnp.take_along_axis(
        positions, jnp.broadcast_to(skeleton[None], (3, box_count, skel_count)), axis=2
    ).reshape(3, box_count * skel_count)
    slot_live = jnp.arange(slot_count, dtype=jnp.int32)[None, :] < near_count[:, None]
    every_box = jnp.arange(total_boxes, dtype=jnp.int32)
    box_listed = jnp.any(
        (near_boxes[:, :, None] == every_box[None, None, :]) & slot_live[:, :, None], axis=1
    )
    target_weight = jnp.repeat(1.0 - box_listed.astype(jnp.float32), skel_count, axis=0)
    payload_far = jnp.concatenate(
        [charges.reshape(2 * columns, box_count * skel_count), skel_pos], axis=0
    )
    zero_phi = jnp.zeros((2, columns, box_count * skel_count), jnp.float32)
    potentials = far_fold(
        skel_count,
        skel_pos,
        target_weight,
        zero_phi,
        lax.all_gather(payload_far, "box", axis=1, tiled=True),
    )
    potentials = potentials.reshape(2, columns, box_count, skel_count)
    far_field = jnp.einsum("bkq,pcbk->pcbq", interp, potentials, precision=HIGHEST)
    applied = 0.5 * current + (near_field + far_field).reshape(2, columns, box_count * points)
    rows_basis, rows_applied = (
        lax.all_to_all(basis, "col", split_axis=3, concat_axis=2, tiled=True),
        lax.all_to_all(applied[None], "col", split_axis=3, concat_axis=2, tiled=True),
    )
    rows_applied = rows_applied[0]
    all_columns = rows_applied.shape[1]
    row_total = rows_applied.shape[2] * lax.axis_size("box") * lax.axis_size("col")
    part_coupling = (
        jnp.einsum("kpiq,pjq->kij", rows_basis, rows_applied, precision=HIGHEST) / row_total
    )
    coupling = lax.psum(part_coupling, ("box", "col"))
    residual = rows_applied - jnp.einsum("kpiq,kij->pjq", rows_basis, coupling, precision=HIGHEST)
    part_gram = jnp.einsum("piq,pjq->ij", residual, residual, precision=HIGHEST) / row_total
    gram_matrix = lax.psum(part_gram, ("box", "col"))
    identity = jnp.eye(all_columns, dtype=jnp.float32)
    shift_term = SHIFT_SCALE * jnp.trace(gram_matrix) / all_columns + EPSILON
    lower_factor = jnp.linalg.cholesky(gram_matrix + shift_term * identity)
    inverse = jax.scipy.linalg.solve_triangular(lower_factor, identity, lower=True)
    normalized = jnp.einsum("ij,pjq->piq", inverse, residual, precision=HIGHEST)
    new_block = lax.all_to_all(normalized, "col", split_axis=1, concat_axis=2, tiled=True)
    return (new_block, coupling, lower_factor.T)


def solution(mesh):
    return jax.shard_map(
        shards,
        mesh=mesh,
        in_specs=(
            P(None, None, "col", "box"),
            P(None, "box"),
            P("box"),
            P("box", None, None),
            P("box", None),
            P("box", None),
            P("box"),
        ),
        out_specs=(P(None, "col", "box"), P(), P()),
        check_vma=False,
    )
```

profile of v0, /device:TPU:8, one launch (start us, length us, event | category | flops | bytes accessed | tf_op | source)
XLA Modules:
  0.0 589.9 jit_solution(7123391067058255241)
XLA Ops:
  9.8 1.9 collective-permute-start
  11.7 3.6 collective-permute-start.1
  18.5 3.8 gather_fusion.1
  24.4 2.3 reshape.851
  26.7 4.3 all-to-all-start.1
  31.5 71.1 %while.32 = (s32[]{:T(128)}, f32[2,16,4,128]{3,1,2,0:T(8,128)S(1)}, s32[4,27]{0,1:T(8,128)S(1)}, s32[]{:T(128)}, f32[35,12,128]{2,0,1:T(8,128)S(1)}, /*index=5*/...) while((s32[]{:T(128)}, f32[2,16,4,128]{3,1,2,0:T(8,128)S(1)}, ...), condition=%wide.region_1.2_spmd.clone, body=%wide.region_0.1_spmd.clone.sunk | while | flops 51481128 | bytes 2097387 | solution.py:110
  102.6 8.3 %all-gather.2.cloned.1.call-done = f32[35,16384]{1,0:T(8,128)} async-done(((f32[35,128]{1,0:T(8,128)}), f32[35,16384]{1,0:T(8,128)}) %all-gather.2.cloned.1.call-update) | async-done | bytes 2293776 | tf_op jit(solution)/shard_map/all_gather | solution.py:132
  110.9 73.7 %while.33 = (s32[]{:T(128)}, f32[2,16,128]{2,1,0:T(8,128)S(1)}, f32[35,16384]{1,0:T(8,128)}, f32[3,128]{1,0:T(4,128)S(1)}, f32[128,512]{0,1:T(8,128)S(1)}, /*ind...) while((s32[]{:T(128)}, f32[2,16,128]{2,1,0:T(8,128)S(1)}, ...), condition=%wide.region_4.5_spmd.clone, body=%wide.region_3.4_spmd.clone.sunk | while | flops 206061600 | bytes 9483192 | solution.py:77
  112.5 4.7 multiply_multiply_fusion.3
  118.1 1.9 fusion.58
  121.7 4.7 multiply_multiply_fusion.3
  127.3 1.9 fusion.58
  130.9 4.7 multiply_multiply_fusion.3
  136.6 1.9 fusion.58
  140.1 4.7 multiply_multiply_fusion.3
  145.8 1.9 fusion.58
  149.3 4.7 multiply_multiply_fusion.3
  155.0 1.9 fusion.58
  158.6 4.7 multiply_multiply_fusion.3
  164.2 1.9 fusion.58
  167.8 4.7 multiply_multiply_fusion.3
  173.5 1.9 fusion.58
  177.0 4.7 multiply_multiply_fusion.3
  182.7 1.9 fusion.58
  186.7 4.1 all-to-all-start
  200.3 262.5 %all-reduce.2.cloned.1.call-done = f32[4,64,64]{1,2,0:T(8,128)} async-done(((f32[4,64,64]{1,2,0:T(8,128)}), f32[4,64,64]{1,2,0:T(8,128)}) %all-reduce.2.cloned.1.call-update) | async-done | bytes 65552 | tf_op jit(solution)/shard_map/psum | solution.py:147
  464.3 94.6 %psum.15 = f32[64,64]{1,0:T(8,128)S(1)} all-reduce(f32[64,64]{1,0:T(8,128)S(1)} %fusion.18), channel_id=1, replica_groups=mesh['box'=128,'col'=4] {'box','col'}, use_global_device_ids=true, to_apply=%region_6.7 | all-reduce | flops 4096 | bytes 32768 | tf_op jit(solution)/shard_map/psum | solution.py:150
  560.3 5.8 cholesky.18
  567.5 4.9 custom-call.7
  573.5 3.3 all-to-all-start.2
  577.5 1.7 copy.143
  579.1 3.2 all-to-all-done.2
  (505 shorter events, 113.9 us)
Async XLA Ops:
  7.2 15.1 %copy-start = (f32[4,32,128]{2,1,0:T(8,128)S(1)}, f32[4,32,128]{2,1,0:T(8,128)}, u32[]{:S(2)}) copy-start(f32[4,32,128]{2,1,0:T(8,128)} %param.14) | copy-start | bytes 196612
  7.2 103.8 %all-gather.2.cloned.1.call-start = ((), (), s32[]{:S(2)}) async-start(), calls=%async_computation.3 | async-start | bytes 2641920 | tf_op jit(solution)/shard_map/all_gather | solution.py:132
  9.8 21.7 %collective-permute-start = (f32[35,4,128]{2,0,1:T(8,128)S(1)}, f32[35,4,128]{2,0,1:T(8,128)S(1)}, u32[]{:S(2)}, u32[]{:S(2)}) collective-permute-start(f32[35,4,128]{2,0,1:T(8,128)S(1)} %pad_maximum_fusion.1), channel_id=1, source_target_pairs={{0,4},{4,8},{8,12},{12,16},{16,20},{20,24},{24,28},{28,32},{32,36}... | collective-permute-start | bytes 215048 | tf_op jit(solution)/shard_map/ppermute | solution.py:24
  11.7 19.8 %collective-permute-start.1 = (f32[35,4,128]{2,0,1:T(8,128)S(1)}, f32[35,4,128]{2,0,1:T(8,128)S(1)}, u32[]{:S(2)}, u32[]{:S(2)}) collective-permute-start(f32[35,4,128]{2,0,1:T(8,128)S(1)} %pad_maximum_fusion.1), channel_id=1, source_target_pairs={{4,0},{8,4},{12,8},{16,12},{20,16},{24,20},{28,24},{32,28},{36,32}... | collective-permute-start | bytes 215048 | tf_op jit(solution)/shard_map/ppermute | solution.py:26
  18.5 3.9 copy-start.2
  18.5 4.9 copy-start.1
  23.4 7.7 %copy-start.3 = (s32[4,27]{1,0:T(4,128)S(1)}, s32[4,27]{1,0:T(4,128)}, u32[]{:S(2)}) copy-start(s32[4,27]{1,0:T(4,128)} %param.16) | copy-start | bytes 1300
  23.4 7.7 %copy-start.4 = (s32[4]{0:T(128)S(1)}, s32[4]{0:T(128)}, u32[]{:S(2)}) copy-start(s32[4]{0:T(128)} %param.17) | copy-start | bytes 52
  26.7 160.0 %all-to-all-start.1 = ((f32[4,1,16384]{2,1,0:T(1,128)}), f32[4,1,16384]{2,1,0:T(1,128)S(1)}, u32[]{:S(2)}, u32[]{:S(2)}) async-start(f32[4,1,16384]{2,1,0:T(1,128)} %reshape.851), calls=%async_computation.1 | async-start | bytes 524288 | tf_op jit(solution)/shard_map/all_to_all | solution.py:138
  186.7 9.8 %all-to-all-start = ((f32[4,1,4096]{2,1,0:T(1,128)}), f32[4,1,4096]{2,1,0:T(1,128)S(1)}, u32[]{:S(2)}, u32[]{:S(2)}) async-start(f32[4,1,4096]{2,1,0:T(1,128)} %reshape.849), calls=%async_computation | async-start | bytes 131072 | tf_op jit(solution)/shard_map/all_to_all | solution.py:139
  190.8 272.0 %all-reduce.2.cloned.1.call-start = ((), (), s32[]{:S(2)}) async-start(), calls=%async_computation.4 | async-start | bytes 262144 | tf_op jit(solution)/shard_map/psum | solution.py:147
  573.5 8.9 %all-to-all-start.2 = ((f32[2,64,128]{2,0,1:T(2,128)}), f32[2,64,128]{2,0,1:T(2,128)S(1)}, u32[]{:S(2)}, u32[]{:S(2)}) async-start(f32[2,64,128]{2,0,1:T(2,128)} %copy.141), calls=%async_computation.2 | async-start | bytes 131072 | tf_op jit(solution)/shard_map/all_to_all | solution.py:156
Sparse Core Ops, SparseCore 0:
  23.5 87.4 all-gather.1
  199.5 263.3 all-reduce.1
where the time goes:
time: 591 us; the launch traced here: 590 us
  waiting for transfers between devices  275 us (47%)
  blocking collectives  94.6 us (16%)
  other arithmetic  93.7 us (16%)
  local copies, waits for them, and re-layouts  55.6 us (9%)
  matrix products  34.8 us (6%)
  starting transfers between devices  17.3 us (3%)
  between operations  15.1 us (3%)
    psum x1, waiting for transfers between devices, shards(): coupling = lax.psum(part_coupling, ('box', 'col'))  263 us
    psum x1, blocking collectives, shards(): gram_matrix = lax.psum(part_gram, ('box', 'col'))  94.6 us
    mul x8, other arithmetic, far_block(): kernel_re.reshape(target_count, source_boxes, skel_count)  37.5 us
    mul x27, other arithmetic, helmholtz_pair(): jnp.cos(WAVENUMBER * distance) * factor  31.7 us
    dot_general x27, matrix products, near_slot(): jnp.einsum('gbtq,pcbq->gpcbt', stacked, source_val, precision=HIGHEST)  15.9 us
    dot_general x8, matrix products, far_block(): jnp.einsum('gts,pcs->gpct', stacked, charge_rows, precision=HIGHEST)  15.4 us
    gather x27, local copies, waits for them, and re-layouts, near_slot(): picked = jnp.take(extended, listed - first_box + box_count, axis=1)  15 us
  transfers between devices with their start and end apart: 7, of which 4 were waited for; matrix products, arithmetic and copies ran while one was open for 28% of the time, Pallas kernels for 0%

commit v1 on v0

--- a/solution.py
+++ b/solution.py
@@ -144,7 +144,7 @@
     part_coupling = (
         jnp.einsum("kpiq,pjq->kij", rows_basis, rows_applied, precision=HIGHEST) / row_total
     )
-    coupling = lax.psum(part_coupling, ("box", "col"))
+    coupling = lax.psum(lax.psum(part_coupling, "col"), "box")
     residual = rows_applied - jnp.einsum("kpiq,kij->pjq", rows_basis, coupling, precision=HIGHEST)
     part_gram = jnp.einsum("piq,pjq->ij", residual, residual, precision=HIGHEST) / row_total
     gram_matrix = lax.psum(part_gram, ("box", "col"))

time: 591 us -> 567 us (0.959)
  the two profiles are of different devices: /device:TPU:8 before, /device:TPU:1 now
where the time goes in v1:
time: 567 us; the launch traced here: 566 us
  waiting for transfers between devices  247 us (44%)
  blocking collectives  95.3 us (17%)
  other arithmetic  93.7 us (17%)
  local copies, waits for them, and re-layouts  55.6 us (10%)
  matrix products  34.8 us (6%)
  starting transfers between devices  20.8 us (4%)
  between operations  14.8 us (3%)
    psum x2, waiting for transfers between devices, shards(): coupling = lax.psum(lax.psum(part_coupling, 'col'), 'box')  239 us
    psum x1, blocking collectives, shards(): gram_matrix = lax.psum(part_gram, ('box', 'col'))  95.3 us
    mul x8, other arithmetic, far_block(): kernel_re.reshape(target_count, source_boxes, skel_count)  37.5 us
    mul x27, other arithmetic, helmholtz_pair(): jnp.cos(WAVENUMBER * distance) * factor  31.7 us
    dot_general x27, matrix products, near_slot(): jnp.einsum('gbtq,pcbq->gpcbt', stacked, source_val, precision=HIGHEST)  15.9 us
    dot_general x8, matrix products, far_block(): jnp.einsum('gts,pcs->gpct', stacked, charge_rows, precision=HIGHEST)  15.4 us
    gather x27, local copies, waits for them, and re-layouts, near_slot(): picked = jnp.take(extended, listed - first_box + box_count, axis=1)  15 us
  transfers between devices with their start and end apart: 8, of which 5 were waited for; matrix products, arithmetic and copies ran while one was open for 29% of the time, Pallas kernels for 0%

profile of v1, /device:TPU:1, one launch (start us, length us, event | category | flops | bytes accessed | tf_op | source)
XLA Modules:
  0.0 565.5 jit_solution(9630037974180762965)
XLA Ops:
  9.8 4.6 collective-permute-start
  14.4 5.5 collective-permute-start.1
  22.9 3.8 gather_fusion.1
  28.9 2.3 reshape.851
  31.2 3.4 all-to-all-start.1
  35.1 71.1 %while.32 = (s32[]{:T(128)}, f32[2,16,4,128]{3,1,2,0:T(8,128)S(1)}, s32[4,27]{0,1:T(8,128)S(1)}, s32[]{:T(128)}, f32[35,12,128]{2,0,1:T(8,128)S(1)}, /*index=5*/...) while((s32[]{:T(128)}, f32[2,16,4,128]{3,1,2,0:T(8,128)S(1)}, ...), condition=%wide.region_1.2_spmd.clone, body=%wide.region_0.1_spmd.clone.sunk | while | flops 51481128 | bytes 2097387 | solution.py:110
  106.2 6.0 %all-gather.2.cloned.1.call-done = f32[35,16384]{1,0:T(8,128)} async-done(((f32[35,128]{1,0:T(8,128)}), f32[35,16384]{1,0:T(8,128)}) %all-gather.2.cloned.1.call-update) | async-done | bytes 2293776 | tf_op jit(solution)/shard_map/all_gather | solution.py:132
  112.3 73.7 %while.33 = (s32[]{:T(128)}, f32[2,16,128]{2,1,0:T(8,128)S(1)}, f32[35,16384]{1,0:T(8,128)}, f32[3,128]{1,0:T(4,128)S(1)}, f32[128,512]{0,1:T(8,128)S(1)}, /*ind...) while((s32[]{:T(128)}, f32[2,16,128]{2,1,0:T(8,128)S(1)}, ...), condition=%wide.region_4.5_spmd.clone, body=%wide.region_3.4_spmd.clone.sunk | while | flops 206061600 | bytes 9483192 | solution.py:77
  113.8 4.7 multiply_multiply_fusion.3
  119.5 1.9 fusion.58
  123.0 4.7 multiply_multiply_fusion.3
  128.7 1.9 fusion.58
  132.2 4.7 multiply_multiply_fusion.3
  137.9 1.9 fusion.58
  141.5 4.7 multiply_multiply_fusion.3
  147.1 1.9 fusion.58
  150.7 4.7 multiply_multiply_fusion.3
  156.4 1.9 fusion.58
  159.9 4.7 multiply_multiply_fusion.3
  165.6 1.9 fusion.58
  169.1 4.7 multiply_multiply_fusion.3
  174.8 1.9 fusion.58
  178.3 4.7 multiply_multiply_fusion.3
  184.0 1.9 fusion.58
  188.0 3.9 all-to-all-start
  199.4 48.6 %all-reduce.3.cloned.1.call-done = f32[4,64,64]{1,2,0:T(8,128)} async-done(((f32[4,64,64]{1,2,0:T(8,128)}), f32[4,64,64]{1,2,0:T(8,128)}) %all-reduce.3.cloned.1.call-update) | async-done | bytes 65552 | tf_op jit(solution)/shard_map/psum | solution.py:147
  249.0 190.3 %all-reduce.5.cloned.1.call-done = f32[4,64,64]{1,2,0:T(8,128)} async-done(((f32[4,64,64]{1,2,0:T(8,128)}), f32[4,64,64]{1,2,0:T(8,128)}) %all-reduce.5.cloned.1.call-update) | async-done | bytes 65552 | tf_op jit(solution)/shard_map/psum | solution.py:147
  440.7 95.3 %psum.23 = f32[64,64]{1,0:T(8,128)S(1)} all-reduce(f32[64,64]{1,0:T(8,128)S(1)} %fusion.18), channel_id=1, replica_groups=mesh['box'=128,'col'=4] {'box','col'}, use_global_device_ids=true, to_apply=%region_7.8 | all-reduce | flops 4096 | bytes 32768 | tf_op jit(solution)/shard_map/psum | solution.py:150
  537.4 5.8 %cholesky.18 = f32[64,64]{1,0:T(8,128)S(1)} custom-call(f32[64,64]{1,0:T(8,128)S(1)} %fusion.26), custom_call_target="Cholesky" | custom-call | tf_op jit(solution)/shard_map/jit(cholesky)/cholesky | solution.py:153
  544.6 4.9 custom-call.7
  550.6 3.3 all-to-all-start.2
  556.2 2.1 all-to-all-done.2
  (508 shorter events, 114.5 us)
Async XLA Ops:
  7.2 19.6 %copy-start = (f32[4,32,128]{2,1,0:T(8,128)S(1)}, f32[4,32,128]{2,1,0:T(8,128)}, u32[]{:S(2)}) copy-start(f32[4,32,128]{2,1,0:T(8,128)} %param.14) | copy-start | bytes 196612
  7.2 105.1 %all-gather.2.cloned.1.call-start = ((), (), s32[]{:S(2)}) async-start(), calls=%async_computation.3 | async-start | bytes 2641920 | tf_op jit(solution)/shard_map/all_gather | solution.py:132
  9.8 25.3 %collective-permute-start = (f32[35,4,128]{2,0,1:T(8,128)S(1)}, f32[35,4,128]{2,0,1:T(8,128)S(1)}, u32[]{:S(2)}, u32[]{:S(2)}) collective-permute-start(f32[35,4,128]{2,0,1:T(8,128)S(1)} %pad_maximum_fusion.1), channel_id=1, source_target_pairs={{0,4},{4,8},{8,12},{12,16},{16,20},{20,24},{24,28},{28,32},{32,36}... | collective-permute-start | bytes 215048 | tf_op jit(solution)/shard_map/ppermute | solution.py:24
  14.4 20.7 %collective-permute-start.1 = (f32[35,4,128]{2,0,1:T(8,128)S(1)}, f32[35,4,128]{2,0,1:T(8,128)S(1)}, u32[]{:S(2)}, u32[]{:S(2)}) collective-permute-start(f32[35,4,128]{2,0,1:T(8,128)S(1)} %pad_maximum_fusion.1), channel_id=1, source_target_pairs={{4,0},{8,4},{12,8},{16,12},{20,16},{24,20},{28,24},{32,28},{36,32}... | collective-permute-start | bytes 215048 | tf_op jit(solution)/shard_map/ppermute | solution.py:26
  22.9 3.9 copy-start.2
  22.9 4.9 copy-start.1
  27.8 6.8 %copy-start.3 = (s32[4,27]{1,0:T(4,128)S(1)}, s32[4,27]{1,0:T(4,128)}, u32[]{:S(2)}) copy-start(s32[4,27]{1,0:T(4,128)} %param.16) | copy-start | bytes 1300
  27.8 6.9 %copy-start.4 = (s32[4]{0:T(128)S(1)}, s32[4]{0:T(128)}, u32[]{:S(2)}) copy-start(s32[4]{0:T(128)} %param.17) | copy-start | bytes 52
  31.2 156.8 %all-to-all-start.1 = ((f32[4,1,16384]{2,1,0:T(1,128)}), f32[4,1,16384]{2,1,0:T(1,128)S(1)}, u32[]{:S(2)}, u32[]{:S(2)}) async-start(f32[4,1,16384]{2,1,0:T(1,128)} %reshape.851), calls=%async_computation.1 | async-start | bytes 524288 | tf_op jit(solution)/shard_map/all_to_all | solution.py:138
  188.0 8.4 %all-to-all-start = ((f32[4,1,4096]{2,1,0:T(1,128)}), f32[4,1,4096]{2,1,0:T(1,128)S(1)}, u32[]{:S(2)}, u32[]{:S(2)}) async-start(f32[4,1,4096]{2,1,0:T(1,128)} %reshape.849), calls=%async_computation | async-start | bytes 131072 | tf_op jit(solution)/shard_map/all_to_all | solution.py:139
  192.0 56.0 %all-reduce.3.cloned.1.call-start = ((), (), s32[]{:S(2)}) async-start(), calls=%async_computation.4 | async-start | bytes 262144 | tf_op jit(solution)/shard_map/psum | solution.py:147
  199.3 239.9 %all-reduce.5.cloned.1.call-start = ((), (), s32[]{:S(2)}) async-start(), calls=%async_computation.5 | async-start | bytes 262144 | tf_op jit(solution)/shard_map/psum | solution.py:147
  550.6 7.7 %all-to-all-start.2 = ((f32[2,64,128]{2,0,1:T(2,128)}), f32[2,64,128]{2,0,1:T(2,128)S(1)}, u32[]{:S(2)}, u32[]{:S(2)}) async-start(f32[2,64,128]{2,0,1:T(2,128)} %copy.141), calls=%async_computation.2 | async-start | bytes 131072 | tf_op jit(solution)/shard_map/all_to_all | solution.py:156
Sparse Core Ops, SparseCore 0:
  27.9 84.2 all-gather.1
  199.5 48.4 all-reduce.2
  251.2 188.0 all-reduce.4
